TPU v7x, 256 devices: a whole 4x4x8 slice. The times are simulated.
256 devices in a mesh: tm: 32 (over x, y, core), space: 8 (over z).
Axes of the slice: x: 4, y: 4, z: 8, core: 2. Of those that a mesh axis runs over, the one named last changes fastest.
Arguments:
- snapshots: bfloat16 [512, 524288], P('tm', 'space'), may hold values from -6 to 6
- block_lists: int32 [8192, 2], P(('tm', 'space')), may hold values from 0 to 8191
- tile_counts: int32 [8192], P(('tm', 'space')), may hold values from 1 to 2
- remap_weights: bfloat16 [8192, 64, 128], P(('tm', 'space')), may hold values from -0.5 to 0.5
- basis: bfloat16 [524288, 1024], P(('tm', 'space')), may hold values from -6 to 6
- variances: float32 [1024], replicated, may hold values from 0.3 to 3
Outputs:
- coeffs: float32 [1024, 512], P('space')
- rotated: bfloat16 [524288, 1024], P(('tm', 'space'))
Inputs may be any that keep to these rules, and one draw needn't show every extreme that they name: `block_lists`: slots at or beyond a tile's count carry no weight.
All inputs are finite; a program needn't handle non-finite values.
Results may differ from a plain program's by a relative error of at most 0.0043.
Values may be sent and summed in bfloat16 or wider, within the bound.
No kernel may reach another device: no remote copies, remote signals or barrier semaphores. Data moves between devices by JAX's collectives and lax.ppermute only.
A program may use at most 192 MiB of HBM per device.

v0:
```python
import math
import jax
import jax.numpy as jnp
from jax import lax
from jax.sharding import PartitionSpec as P

TILE = 64
MAXB = 2


def per_device(snapshots, block_lists, tile_counts, remap_weights, basis, variances):
    local_tiles = block_lists.shape[0]
    time_rows = snapshots.shape[0]
    tm_size = lax.axis_size("tm")
    list_column, count_column = (
        lax.all_gather(block_lists, "tm", axis=0, tiled=True),
        lax.all_gather(tile_counts, "tm", axis=0, tiled=True),
    )
    gathered = lax.all_gather(snapshots, "space", axis=1, tiled=True)
    cell_total = gathered.shape[1]
    blocks = gathered.reshape(time_rows, cell_total // TILE, TILE)
    picked = blocks[:, list_column.reshape(-1), :].reshape(
        time_rows, tm_size * local_tiles, MAXB * TILE
    )
    slot_index = jnp.arange(MAXB * TILE, dtype=jnp.int32) // TILE
    weight_column = lax.all_gather(remap_weights, "tm", axis=0, tiled=True)
    keep = slot_index[None, :] < count_column[:, None]
    masked = jnp.where(keep[:, None, :], weight_column, jnp.zeros_like(weight_column))
    remap_part = jnp.einsum("kip,tkp->kit", masked, picked, preferred_element_type=jnp.float32)
    remap_part = remap_part.astype(jnp.bfloat16).reshape(tm_size, local_tiles * TILE, time_rows)
    arrived = lax.all_to_all(remap_part, "tm", split_axis=0, concat_axis=2, tiled=True)
    remapped = arrived.reshape(local_tiles * TILE, tm_size * time_rows)
    snap_total = remapped.shape[1]
    partial_coeffs = lax.dot_general(
        basis, remapped, (((0,), (0,)), ((), ())), preferred_element_type=jnp.float32
    )
    coeffs = lax.psum(partial_coeffs, ("tm", "space")) / math.sqrt(cell_total)
    coeff_half = coeffs.astype(jnp.bfloat16)
    coeff_rows = coeffs.shape[0] // lax.axis_size("space")
    own_coeffs = lax.dynamic_slice_in_dim(
        coeffs, lax.axis_index("space") * coeff_rows, coeff_rows, 0
    )
    update = lax.dot_general(
        remapped, coeff_half, (((1,), (1,)), ((), ())), preferred_element_type=jnp.float32
    ) / math.sqrt(snap_total)
    rotated = (basis.astype(jnp.float32) * variances[None, :] + update).astype(jnp.bfloat16)
    return (own_coeffs, rotated)


def solution(mesh):
    return jax.shard_map(
        per_device,
        mesh=mesh,
        in_specs=(
            P("tm", "space"),
            P(("tm", "space"), None),
            P(("tm", "space")),
            P(("tm", "space"), None, None),
            P(("tm", "space"), None),
            P(),
        ),
        out_specs=(P("space", None), P(("tm", "space"), None)),
        check_vma=False,
    )
```

profile of v0, /device:TPU:2, one launch (start us, length us, event | category | flops | bytes accessed | tf_op | source)
XLA Modules:
  0.0 671.5 jit_solution(16009837492111305055)
XLA Ops:
  7.2 0.0 all-gather.6.cloned.1.call-start
  7.2 0.7 all-gather.6.cloned.1.call-update
  7.9 0.0 all-gather.4.cloned.1.call-start
  7.9 0.7 all-gather.4.cloned.1.call-update
  8.6 0.0 all-reduce.3.cloned.1.call-start
  8.7 24.3 %all-gather = s32[32,32,2]{1,2,0:T(2,128)S(1)} all-gather(s32[1,32,2]{1,2,0:T(2,128)} %bitcast.20), channel_id=1, replica_groups=mesh['tm'=32,'space'=8] {'tm'}, dimensions={0}, use_global_device_ids=true | all-gather | bytes 8448 | tf_op jit(solution)/shard_map/all_gather | solution.py:16
  33.0 0.3 copy.16
  33.2 0.3 reshape.86
  33.6 1.3 dynamic-slice
  35.5 0.9 dynamic-update-slice
  36.3 13.8 %all-reduce = s32[1024]{0:T(1024)S(1)} all-reduce(s32[1024]{0:T(1024)S(1)} %dynamic-update-slice), channel_id=1, replica_groups=mesh['tm'=32,'space'=8] {'tm'}, use_global_device_ids=true, to_apply=%add | all-reduce | flops 1024 | bytes 8192
  50.1 0.2 broadcast_compare_fusion
  50.4 135.1 %all-gather.6.cloned.1.call-done = bf16[16,524288]{1,0:T(8,128)(2,1)} async-done(((bf16[16,65536]{1,0:T(8,128)(2,1)}), bf16[16,524288]{1,0:T(8,128)(2,1)}) %all-gather.6.cloned.1.call-update) | async-done | bytes 16777232 | tf_op jit(solution)/shard_map/all_gather | solution.py:19
  185.5 60.5 %reshape.85 = bf16[16,8192,64]{2,1,0:T(8,128)(2,1)} reshape(bf16[16,524288]{1,0:T(8,128)(2,1)} %all-gather.6.cloned.1.call-done) | data formatting | bytes 33554432 | tf_op jit(solution)/shard_map/reshape | solution.py:21
  246.0 29.6 %copy.17 = bf16[16,8192,64]{2,0,1:T(8,128)(2,1)} copy(bf16[16,8192,64]{2,1,0:T(8,128)(2,1)} %reshape.85) | data formatting | bytes 33554432 | tf_op jit(solution)/shard_map/reshape | solution.py:21
  275.6 33.4 %gather_fusion = bf16[2048,16,64]{2,1,0:T(8,128)(2,1)} fusion(bf16[16,8192,64]{2,0,1:T(8,128)(2,1)} %copy.17, s32[2048]{0:T(1024)S(1)} %broadcast_clamp_fusion), kind=kCustom, calls=%fused_computation | custom fusion | bytes 8396800 | tf_op jit(solution)/shard_map/gather | solution.py:22
  309.0 8.8 %copy.18 = bf16[16,2048,64]{2,1,0:T(8,128)(2,1)} copy(bf16[16,2048,64]{2,0,1:T(8,128)(2,1)} %bitcast.16) | data formatting | bytes 8388608 | tf_op jit(solution)/shard_map/gather | solution.py:22
  317.8 11.3 %reshape.87 = bf16[16,1024,128]{2,1,0:T(8,128)(2,1)} reshape(bf16[16,2048,64]{2,1,0:T(8,128)(2,1)} %copy.18) | data formatting | bytes 8388608 | tf_op jit(solution)/shard_map/reshape | solution.py:22
  329.1 0.0 all-gather.4.cloned.1.call-done
  329.1 14.3 %fusion.5 = bf16[1024,64,16]{1,2,0:T(8,128)(2,1)} fusion(bf16[16,1024,128]{2,1,0:T(8,128)(2,1)} %reshape.87, bf16[1024,64,128]{2,1,0:T(8,128)(2,1)} %all-gather.4.cloned.1.call-done, pred[1024,128]{1,0:T(8,128)(4,1)S(1)} %broadcast_compare_fusion), kind=kOutput, calls=%fused_computation.7 | convolution fusion | flops 277872640 | bytes 23199744 | tf_op jit(solution)/shard_map/kip,tkp->kit/dot_general | solution.py:29
  343.3 5.3 copy.20
  348.6 5.8 reshape.88
  354.4 0.0 copy-start
  354.4 1.2 copy.21
  355.5 32.6 %all_to_all.15 = bf16[32,2048,16]{1,2,0:T(8,128)(2,1)S(1)} all-to-all(bf16[32,2048,16]{1,2,0:T(8,128)(2,1)S(1)} %copy.21), channel_id=1, replica_groups=mesh['tm'=32,'space'=8] {'tm'}, dimensions={0} | all-to-all | bytes 4194304 | tf_op jit(solution)/shard_map/all_to_all | solution.py:31
  388.2 0.0 copy-done
  388.2 3.7 convolution_bitcast_fusion
  391.9 0.0 copy-start.1
  391.9 0.0 all-reduce.3.cloned.1.call-update
  391.9 262.6 %all-reduce.3.cloned.1.call-done = f32[1024,512]{0,1:T(8,128)} async-done(((f32[1024,512]{0,1:T(8,128)}), f32[1024,512]{0,1:T(8,128)}) %all-reduce.3.cloned.1.call-update) | async-done | bytes 2097168 | tf_op jit(solution)/shard_map/psum | solution.py:37
  654.6 1.8 broadcast_multiply_fusion
  656.4 0.8 copy.22
  657.3 0.0 copy-done.1
  657.3 7.7 %add_convert_fusion = bf16[2048,1024]{1,0:T(8,128)(2,1)} fusion(bf16[2048,1024]{1,0:T(8,128)(2,1)} %param.10, bf16[2048,512]{0,1:T(8,128)(2,1)S(1)} %bitcast.18, f32[1024]{0:T(1024)S(1)} %copy-done.1, f32[1024,512]{0,1:T(8,128)} %all-reduce.3.cloned.1.call-done), kind=kOutput, calls=%fused_computation.4 | convolution fusion | flops 2159017984 | bytes 12587008 | tf_op jit(solution)/shard_map/dot_general | solution.py:43
  (5 shorter events, 0.1 us)
Async XLA Ops:
  7.2 178.3 %all-gather.6.cloned.1.call-start = ((), (), s32[]{:S(2)}) async-start(), calls=%async_computation.2 | async-start | bytes 18874368 | tf_op jit(solution)/shard_map/all_gather | solution.py:19
  7.9 321.2 %all-gather.4.cloned.1.call-start = ((), (), s32[]{:S(2)}) async-start(), calls=%async_computation.1 | async-start | bytes 17301504 | tf_op jit(solution)/shard_map/all_gather | solution.py:26
  8.6 645.9 %all-reduce.3.cloned.1.call-start = ((), (), s32[]{:S(2)}) async-start(), calls=%async_computation.3 | async-start | bytes 4194304 | tf_op jit(solution)/shard_map/psum | solution.py:37
  354.4 33.8 %copy-start = (bf16[2048,1024]{1,0:T(8,128)(2,1)S(1)}, bf16[2048,1024]{1,0:T(8,128)(2,1)}, u32[]{:S(2)}) copy-start(bf16[2048,1024]{1,0:T(8,128)(2,1)} %param.10) | copy-start | bytes 12582916
  391.9 265.4 %copy-start.1 = (f32[1024]{0:T(1024)S(1)}, f32[1024]{0:T(1024)}, u32[]{:S(2)}) copy-start(f32[1024]{0:T(1024)} %param.11) | copy-start | bytes 12292
Sparse Core Ops, SparseCore 0:
  9.8 175.6 all-gather.5
  188.0 76.1 all-gather.3
  392.0 262.4 all-reduce.2
where the time goes:
time: 673 us; the launch traced here: 671 us
  waiting for transfers between devices  399 us (59%)
  local copies, waits for them, and re-layouts  159 us (24%)
  blocking collectives  70.7 us (11%)
  matrix products  25.6 us (4%)
  between operations  14.5 us (2%)
    psum x1, waiting for transfers between devices, per_device(): coeffs = lax.psum(partial_coeffs, ('tm', 'space')) / math.sqrt(cell_total)  263 us
    all_gather x1, waiting for transfers between devices, per_device(): gathered = lax.all_gather(snapshots, 'space', axis=1, tiled=True)  135 us
    reshape x2, local copies, waits for them, and re-layouts, per_device(): blocks = gathered.reshape(time_rows, cell_total // TILE, TILE)  90.1 us
    gather x2, local copies, waits for them, and re-layouts, per_device(): blocks[:, list_column.reshape(-1), :]  42.2 us
    all_to_all x1, blocking collectives, per_device(): lax.all_to_all(remap_part, 'tm', split_axis=0, concat_axis=2, tiled=True)  32.6 us
    all_gather x1, blocking collectives, per_device(): lax.all_gather(block_lists, 'tm', axis=0, tiled=True)  24.3 us
    dot_general x1, matrix products, per_device(): jnp.einsum('kip,tkp->kit', masked, picked, preferred_element_type=jnp.flo...  14.3 us
    unnamed x1, blocking collectives  13.8 us
  transfers between devices with their start and end apart: 3, of which 2 were waited for; matrix products, arithmetic and copies ran while one was open for 22% of the time, Pallas kernels for 0%

commit v1 on v0

--- a/solution.py
+++ b/solution.py
@@ -34,7 +34,7 @@
     partial_coeffs = lax.dot_general(
         basis, remapped, (((0,), (0,)), ((), ())), preferred_element_type=jnp.float32
     )
-    coeffs = lax.psum(partial_coeffs, ("tm", "space")) / math.sqrt(cell_total)
+    coeffs = lax.psum(lax.psum(partial_coeffs, "space"), "tm") / math.sqrt(cell_total)
     coeff_half = coeffs.astype(jnp.bfloat16)
     coeff_rows = coeffs.shape[0] // lax.axis_size("space")
     own_coeffs = lax.dynamic_slice_in_dim(

time: 673 us -> 612 us (0.909)
  waiting for transfers between devices: 399 us -> 336 us
    psum x1 -> x2, waiting for transfers between devices: 263 us -> 200 us  [the longest x1 119 us: per_device(): lax.psum(lax.psum(partial_coeffs, 'space'), 'tm') / math.sqrt(cell_total)]
  transfers between devices with their start and end apart: 3 -> 4, of which waited for: 2 -> 3; matrix products, arithmetic and copies ran while one was open for 22% -> 24% of each run, Pallas kernels for 0% -> 0%
where the time goes in v1:
time: 612 us; the launch traced here: 609 us
  waiting for transfers between devices  336 us (55%)
  local copies, waits for them, and re-layouts  159 us (26%)
  blocking collectives  70.7 us (12%)
  matrix products  25.6 us (4%)
  between operations  14.5 us (2%)
    all_gather x1, waiting for transfers between devices, per_device(): gathered = lax.all_gather(snapshots, 'space', axis=1, tiled=True)  135 us
    psum x1, waiting for transfers between devices, per_device(): lax.psum(lax.psum(partial_coeffs, 'space'), 'tm') / math.sqrt(cell_total)  119 us
    reshape x2, local copies, waits for them, and re-layouts, per_device(): blocks = gathered.reshape(time_rows, cell_total // TILE, TILE)  90.1 us
    psum x1, waiting for transfers between devices, per_device(): lax.psum(partial_coeffs, 'space')  80.7 us
    gather x2, local copies, waits for them, and re-layouts, per_device(): blocks[:, list_column.reshape(-1), :]  42.2 us
    all_to_all x1, blocking collectives, per_device(): lax.all_to_all(remap_part, 'tm', split_axis=0, concat_axis=2, tiled=True)  32.6 us
    all_gather x1, blocking collectives, per_device(): lax.all_gather(block_lists, 'tm', axis=0, tiled=True)  24.3 us
    dot_general x1, matrix products, per_device(): jnp.einsum('kip,tkp->kit', masked, picked, preferred_element_type=jnp.flo...  14.3 us
  transfers between devices with their start and end apart: 4, of which 3 were waited for; matrix products, arithmetic and copies ran while one was open for 24% of the time, Pallas kernels for 0%

profile of v1, /device:TPU:2, one launch (start us, length us, event | category | flops | bytes accessed | tf_op | source)
XLA Modules:
  0.0 609.0 jit_solution(17740730186345002430)
XLA Ops:
  7.2 0.0 all-gather.6.cloned.1.call-start
  7.2 0.7 all-gather.6.cloned.1.call-update
  7.9 0.0 all-gather.4.cloned.1.call-start
  7.9 0.7 all-gather.4.cloned.1.call-update
  8.6 0.0 all-reduce.4.cloned.1.call-start
  8.7 24.3 %all-gather = s32[32,32,2]{1,2,0:T(2,128)S(1)} all-gather(s32[1,32,2]{1,2,0:T(2,128)} %bitcast.20), channel_id=1, replica_groups=mesh['tm'=32,'space'=8] {'tm'}, dimensions={0}, use_global_device_ids=true | all-gather | bytes 8448 | tf_op jit(solution)/shard_map/all_gather | solution.py:16
  33.0 0.3 copy.16
  33.2 0.3 reshape.86
  33.6 1.3 dynamic-slice
  35.5 0.9 dynamic-update-slice
  36.3 13.8 %all-reduce = s32[1024]{0:T(1024)S(1)} all-reduce(s32[1024]{0:T(1024)S(1)} %dynamic-update-slice), channel_id=1, replica_groups=mesh['tm'=32,'space'=8] {'tm'}, use_global_device_ids=true, to_apply=%add | all-reduce | flops 1024 | bytes 8192
  50.1 0.2 broadcast_compare_fusion
  50.4 135.1 %all-gather.6.cloned.1.call-done = bf16[16,524288]{1,0:T(8,128)(2,1)} async-done(((bf16[16,65536]{1,0:T(8,128)(2,1)}), bf16[16,524288]{1,0:T(8,128)(2,1)}) %all-gather.6.cloned.1.call-update) | async-done | bytes 16777232 | tf_op jit(solution)/shard_map/all_gather | solution.py:19
  185.5 60.5 %reshape.85 = bf16[16,8192,64]{2,1,0:T(8,128)(2,1)} reshape(bf16[16,524288]{1,0:T(8,128)(2,1)} %all-gather.6.cloned.1.call-done) | data formatting | bytes 33554432 | tf_op jit(solution)/shard_map/reshape | solution.py:21
  246.0 29.6 %copy.17 = bf16[16,8192,64]{2,0,1:T(8,128)(2,1)} copy(bf16[16,8192,64]{2,1,0:T(8,128)(2,1)} %reshape.85) | data formatting | bytes 33554432 | tf_op jit(solution)/shard_map/reshape | solution.py:21
  275.6 33.4 %gather_fusion = bf16[2048,16,64]{2,1,0:T(8,128)(2,1)} fusion(bf16[16,8192,64]{2,0,1:T(8,128)(2,1)} %copy.17, s32[2048]{0:T(1024)S(1)} %broadcast_clamp_fusion), kind=kCustom, calls=%fused_computation | custom fusion | bytes 8396800 | tf_op jit(solution)/shard_map/gather | solution.py:22
  309.0 8.8 %copy.18 = bf16[16,2048,64]{2,1,0:T(8,128)(2,1)} copy(bf16[16,2048,64]{2,0,1:T(8,128)(2,1)} %bitcast.16) | data formatting | bytes 8388608 | tf_op jit(solution)/shard_map/gather | solution.py:22
  317.8 11.3 %reshape.87 = bf16[16,1024,128]{2,1,0:T(8,128)(2,1)} reshape(bf16[16,2048,64]{2,1,0:T(8,128)(2,1)} %copy.18) | data formatting | bytes 8388608 | tf_op jit(solution)/shard_map/reshape | solution.py:22
  329.1 0.0 all-gather.4.cloned.1.call-done
  329.1 14.3 %fusion.5 = bf16[1024,64,16]{1,2,0:T(8,128)(2,1)} fusion(bf16[16,1024,128]{2,1,0:T(8,128)(2,1)} %reshape.87, bf16[1024,64,128]{2,1,0:T(8,128)(2,1)} %all-gather.4.cloned.1.call-done, pred[1024,128]{1,0:T(8,128)(4,1)S(1)} %broadcast_compare_fusion), kind=kOutput, calls=%fused_computation.7 | convolution fusion | flops 277872640 | bytes 23199744 | tf_op jit(solution)/shard_map/kip,tkp->kit/dot_general | solution.py:29
  343.3 5.3 copy.20
  348.6 5.8 reshape.88
  354.4 0.0 copy-start
  354.4 1.2 copy.21
  355.5 32.6 %all_to_all.15 = bf16[32,2048,16]{1,2,0:T(8,128)(2,1)S(1)} all-to-all(bf16[32,2048,16]{1,2,0:T(8,128)(2,1)S(1)} %copy.21), channel_id=1, replica_groups=mesh['tm'=32,'space'=8] {'tm'}, dimensions={0} | all-to-all | bytes 4194304 | tf_op jit(solution)/shard_map/all_to_all | solution.py:31
  388.2 0.0 copy-done
  388.2 3.7 convolution_bitcast_fusion
  391.9 0.0 all-reduce.4.cloned.1.call-update
  391.9 0.0 copy-start.1
  391.9 0.3 all-reduce.6.cloned.1.call-start
  392.2 80.7 %all-reduce.4.cloned.1.call-done = f32[1024,512]{0,1:T(8,128)} async-done(((f32[1024,512]{0,1:T(8,128)}), f32[1024,512]{0,1:T(8,128)}) %all-reduce.4.cloned.1.call-update) | async-done | bytes 2097168 | tf_op jit(solution)/shard_map/psum | solution.py:37
  472.9 0.0 all-reduce.6.cloned.1.call-update
  472.9 119.1 %all-reduce.6.cloned.1.call-done = f32[1024,512]{0,1:T(8,128)} async-done(((f32[1024,512]{0,1:T(8,128)}), f32[1024,512]{0,1:T(8,128)}) %all-reduce.6.cloned.1.call-update) | async-done | bytes 2097168 | tf_op jit(solution)/shard_map/psum | solution.py:37
  592.0 1.8 broadcast_multiply_fusion
  593.9 0.8 copy.22
  594.7 0.0 copy-done.1
  594.7 7.7 %add_convert_fusion = bf16[2048,1024]{1,0:T(8,128)(2,1)} fusion(bf16[2048,1024]{1,0:T(8,128)(2,1)} %param.10, bf16[2048,512]{0,1:T(8,128)(2,1)S(1)} %bitcast.18, f32[1024]{0:T(1024)S(1)} %copy-done.1, f32[1024,512]{0,1:T(8,128)} %all-reduce.6.cloned.1.call-done), kind=kOutput, calls=%fused_computation.4 | convolution fusion | flops 2159017984 | bytes 12587008 | tf_op jit(solution)/shard_map/dot_general | solution.py:43
  (5 shorter events, 0.1 us)
Async XLA Ops:
  7.2 178.3 %all-gather.6.cloned.1.call-start = ((), (), s32[]{:S(2)}) async-start(), calls=%async_computation.2 | async-start | bytes 18874368 | tf_op jit(solution)/shard_map/all_gather | solution.py:19
  7.9 321.2 %all-gather.4.cloned.1.call-start = ((), (), s32[]{:S(2)}) async-start(), calls=%async_computation.1 | async-start | bytes 17301504 | tf_op jit(solution)/shard_map/all_gather | solution.py:26
  8.6 464.3 %all-reduce.4.cloned.1.call-start = ((), (), s32[]{:S(2)}) async-start(), calls=%async_computation.3 | async-start | bytes 4194304 | tf_op jit(solution)/shard_map/psum | solution.py:37
  354.4 33.8 %copy-start = (bf16[2048,1024]{1,0:T(8,128)(2,1)S(1)}, bf16[2048,1024]{1,0:T(8,128)(2,1)}, u32[]{:S(2)}) copy-start(bf16[2048,1024]{1,0:T(8,128)(2,1)} %param.10) | copy-start | bytes 12582916
  391.9 202.8 %copy-start.1 = (f32[1024]{0:T(1024)S(1)}, f32[1024]{0:T(1024)}, u32[]{:S(2)}) copy-start(f32[1024]{0:T(1024)} %param.11) | copy-start | bytes 12292
  391.9 200.1 %all-reduce.6.cloned.1.call-start = ((), (), s32[]{:S(2)}) async-start(), calls=%async_computation.4 | async-start | bytes 4194304 | tf_op jit(solution)/shard_map/psum | solution.py:37
Sparse Core Ops, SparseCore 0:
  9.8 175.6 all-gather.5
  188.0 76.1 all-gather.3
  392.0 80.8 all-reduce.3
  476.0 115.9 all-reduce.5
